TPU v7x, 32 devices: a whole 2x2x4 slice. The times are simulated.
32 devices in a mesh: fsdp: 4 (over z), ctx: 2 (over x), tp: 4 (over y, core).
Axes of the slice: x: 2, y: 2, z: 4, core: 2. Of those that a mesh axis runs over, the one named last changes fastest.
Arguments:
- layer_in: bfloat16 [8, 1024, 1024], P('fsdp', ('ctx', 'tp')), may hold values from -6 to 6
- attn_gain: bfloat16 [1024], replicated, may hold values from 0.5 to 1.5
- ffn_gain: bfloat16 [1024], replicated, may hold values from 0.5 to 1.5
- query_weight: bfloat16 [1024, 1024], P(('fsdp', 'ctx'), 'tp'), may hold values from -0.1875 to 0.1875
- key_weight: bfloat16 [1024, 1024], P(('fsdp', 'ctx'), 'tp'), may hold values from -0.1875 to 0.1875
- value_weight: bfloat16 [1024, 1024], P(('fsdp', 'ctx'), 'tp'), may hold values from -0.1875 to 0.1875
- out_weight: bfloat16 [1024, 1024], P(('fsdp', 'ctx'), 'tp'), may hold values from -0.75 to 0.75
- variate_bias: float32 [2, 16], P(None, 'tp'), may hold values from -4 to 4
- gate_weight: bfloat16 [1024, 4096], P(('fsdp', 'ctx'), 'tp'), may hold values from -0.1875 to 0.1875
- up_weight: bfloat16 [1024, 4096], P(('fsdp', 'ctx'), 'tp'), may hold values from -0.1875 to 0.1875
- down_weight: bfloat16 [1024, 4096], P(('fsdp', 'ctx'), 'tp'), may hold values from -0.09375 to 0.09375
- segment_ids: int32 [8, 1024], P('fsdp'), may hold values from 0 to 15, never falling along the last dimension, each value on 1 to 512 neighbouring positions
- variate_ids: int32 [8, 1024], P('fsdp'), may hold values from 0 to 3
- time_ids: int32 [8, 1024], P('fsdp'), may hold values from 0 to 1023
- out_grad: bfloat16 [8, 1024, 1024], P('fsdp', ('ctx', 'tp')), may hold values from -6 to 6
Outputs:
- layer_out: bfloat16 [8, 1024, 1024], P('fsdp', ('ctx', 'tp'))
- in_grad: bfloat16 [8, 1024, 1024], P('fsdp', ('ctx', 'tp'))
- attn_gain_grad: float32 [1024], replicated
- ffn_gain_grad: float32 [1024], replicated
- query_grad: float32 [1024, 1024], P(('fsdp', 'ctx'), 'tp')
- key_grad: float32 [1024, 1024], P(('fsdp', 'ctx'), 'tp')
- value_grad: float32 [1024, 1024], P(('fsdp', 'ctx'), 'tp')
- out_weight_grad: float32 [1024, 1024], P(('fsdp', 'ctx'), 'tp')
- bias_grad: float32 [2, 16], P(None, 'tp')
- gate_grad: float32 [1024, 4096], P(('fsdp', 'ctx'), 'tp')
- up_grad: float32 [1024, 4096], P(('fsdp', 'ctx'), 'tp')
- down_grad: float32 [1024, 4096], P(('fsdp', 'ctx'), 'tp')
All inputs are finite; a program needn't handle non-finite values.
Results may differ from a plain program's by a relative error of at most 0.019.
Values may be sent and summed in bfloat16 or wider, within the bound.
No kernel may reach another device: no remote copies, remote signals or barrier semaphores. Data moves between devices by JAX's collectives and lax.ppermute only.
A program may use at most 128 MiB of HBM per device.

v0:
```python
import jax
import jax.numpy as jnp
from jax import lax
from jax.sharding import PartitionSpec as P

HEADS = 16
HEAD = 64
EPS = 1e-05
NEG = -1e30


def rms_norm(values, gain):
    return values * lax.rsqrt(jnp.mean(values * values, axis=-1, keepdims=True) + EPS) * gain


def rotate(values, time_rows):
    half_dim = values.shape[-1] // 2
    frequency = 10000.0 ** (-2.0 * jnp.arange(half_dim, dtype=jnp.float32) / values.shape[-1])
    angles = time_rows.astype(jnp.float32)[..., None, None] * frequency
    cosine = jnp.cos(angles)
    sine_part = jnp.sin(angles)
    first_half = values[..., :half_dim]
    second = values[..., half_dim:]
    return jnp.concatenate(
        [first_half * cosine - second * sine_part, second * cosine + first_half * sine_part],
        axis=-1,
    )


def swiglu(gate_vals, up_vals):
    return jax.nn.silu(gate_vals) * up_vals


def gather_rows(values):
    return lax.all_gather(values, "tp", axis=1, tiled=True)


def scatter_rows(values):
    return lax.psum_scatter(values, "tp", scatter_dimension=1, tiled=True)


def shards(
    layer_in,
    attn_gain,
    ffn_gain,
    query_weight,
    key_weight,
    value_weight,
    out_weight,
    variate_bias,
    gate_weight,
    up_weight,
    down_weight,
    segment_ids,
    variate_ids,
    time_ids,
    out_grad,
):
    seq_count, share, width = layer_in.shape
    span = share * lax.axis_size("tp")
    seq_length = segment_ids.shape[1]
    offset = lax.axis_index("ctx") * span
    local_heads = variate_bias.shape[1]
    proj_width = local_heads * HEAD
    row_count = seq_count * span
    block = 512
    block_starts = jnp.arange(span // block, dtype=jnp.int32) * block
    scale = HEAD ** (-0.5)
    my_times = lax.dynamic_slice_in_dim(time_ids, offset, span, 1)
    my_variates = lax.dynamic_slice_in_dim(variate_ids, offset, span, 1)
    my_segments = lax.dynamic_slice_in_dim(segment_ids, offset, span, 1)
    bias_same = variate_bias[0]
    bias_diff = variate_bias[1]
    gain_one = attn_gain.astype(jnp.float32)
    gain_two = ffn_gain.astype(jnp.float32)
    inputs = layer_in.astype(jnp.float32)
    rows_one = gather_rows(rms_norm(inputs, gain_one).astype(jnp.bfloat16)).reshape(
        row_count, width
    )
    query_full, key_full, value_full, out_full = (
        lax.all_gather(query_weight, ("fsdp", "ctx"), axis=0, tiled=True),
        lax.all_gather(key_weight, ("fsdp", "ctx"), axis=0, tiled=True),
        lax.all_gather(value_weight, ("fsdp", "ctx"), axis=0, tiled=True),
        lax.all_gather(out_weight, ("fsdp", "ctx"), axis=0, tiled=True),
    )
    queries_raw = jnp.dot(rows_one, query_full, preferred_element_type=jnp.float32).reshape(
        seq_count, span, local_heads, HEAD
    )
    keys_raw = jnp.dot(rows_one, key_full, preferred_element_type=jnp.float32).reshape(
        seq_count, span, local_heads, HEAD
    )
    queries = rotate(queries_raw, my_times).astype(jnp.bfloat16)
    keys_mine = rotate(keys_raw, my_times).astype(jnp.bfloat16).reshape(seq_count, span, proj_width)
    values_mine = (
        jnp.dot(rows_one, value_full, preferred_element_type=jnp.float32)
        .astype(jnp.bfloat16)
        .reshape(seq_count, span, proj_width)
    )
    keys_all, values_all = (
        lax.all_gather(keys_mine, "ctx", axis=1, tiled=True),
        lax.all_gather(values_mine, "ctx", axis=1, tiled=True),
    )

    def scores_of(query_block, key_rows, query_var, key_var, query_seg, key_seg):
        raw = (
            jnp.einsum("qhd,khd->hqk", query_block, key_rows, preferred_element_type=jnp.float32)
            * scale
        )
        same = (query_var[:, None] == key_var[None, :])[None]
        raw = raw + jnp.where(same, bias_same[:, None, None], bias_diff[:, None, None])
        return (jnp.where((query_seg[:, None] == key_seg[None, :])[None], raw, NEG), same)

    mixed_parts = []
    lse_parts = []
    for seq in range(seq_count):
        key_rows = keys_all[seq].reshape(seq_length, local_heads, HEAD)
        value_rows = values_all[seq].reshape(seq_length, local_heads, HEAD)

        def forward_block(first, seq=seq, key_rows=key_rows, value_rows=value_rows):
            query_block = queries[seq]
            query_var = my_variates[seq]
            query_seg = my_segments[seq]
            scores, same = scores_of(
                query_block, key_rows, query_var, variate_ids[seq], query_seg, segment_ids[seq]
            )
            top = jnp.max(scores, axis=-1, keepdims=True)
            expo = jnp.exp(scores - top)
            total = jnp.sum(expo, axis=-1, keepdims=True)
            probs = (expo / total).astype(jnp.bfloat16)
            mixed_block = jnp.einsum(
                "hqk,khd->qhd", probs, value_rows, preferred_element_type=jnp.float32
            )
            return (
                mixed_block.astype(jnp.bfloat16).reshape(block, proj_width),
                top[..., 0] + jnp.log(total[..., 0]),
            )

        mixed_seq, lse_seq = lax.map(forward_block, block_starts)
        mixed_parts.append(mixed_seq.reshape(span, proj_width))
        lse_parts.append(lse_seq)
    mixed = jnp.stack(mixed_parts).reshape(row_count, proj_width)
    attn_part = jnp.einsum("rp,dp->rd", mixed, out_full, preferred_element_type=jnp.float32)
    hidden = inputs + scatter_rows(attn_part.reshape(seq_count, span, width))
    rows_two = gather_rows(rms_norm(hidden, gain_two).astype(jnp.bfloat16)).reshape(
        row_count, width
    )
    gate_full, up_full, down_full = (
        lax.all_gather(gate_weight, ("fsdp", "ctx"), axis=0, tiled=True),
        lax.all_gather(up_weight, ("fsdp", "ctx"), axis=0, tiled=True),
        lax.all_gather(down_weight, ("fsdp", "ctx"), axis=0, tiled=True),
    )
    gate = jnp.dot(rows_two, gate_full, preferred_element_type=jnp.float32)
    up_vals = jnp.dot(rows_two, up_full, preferred_element_type=jnp.float32)
    act = swiglu(gate, up_vals).astype(jnp.bfloat16)
    ffn_part = jnp.einsum("rf,df->rd", act, down_full, preferred_element_type=jnp.float32)
    layer_out = (hidden + scatter_rows(ffn_part.reshape(seq_count, span, width))).astype(
        jnp.bfloat16
    )
    query_back, key_back, value_back, out_back = (
        lax.all_gather(query_weight, ("fsdp", "ctx"), axis=0, tiled=True),
        lax.all_gather(key_weight, ("fsdp", "ctx"), axis=0, tiled=True),
        lax.all_gather(value_weight, ("fsdp", "ctx"), axis=0, tiled=True),
        lax.all_gather(out_weight, ("fsdp", "ctx"), axis=0, tiled=True),
    )
    gate_back, up_back, down_back = (
        lax.all_gather(gate_weight, ("fsdp", "ctx"), axis=0, tiled=True),
        lax.all_gather(up_weight, ("fsdp", "ctx"), axis=0, tiled=True),
        lax.all_gather(down_weight, ("fsdp", "ctx"), axis=0, tiled=True),
    )
    grad_rows = gather_rows(out_grad).reshape(row_count, width)
    d_act = jnp.dot(grad_rows, down_back, preferred_element_type=jnp.float32)
    down_local = jnp.einsum("rd,rf->df", grad_rows, act, preferred_element_type=jnp.float32)
    swiglu_pull = jax.vjp(swiglu, gate, up_vals)[1]
    d_gate, d_up = swiglu_pull(d_act)
    d_gate = d_gate.astype(jnp.bfloat16)
    d_up = d_up.astype(jnp.bfloat16)
    gate_local = jnp.einsum("rd,rf->df", rows_two, d_gate, preferred_element_type=jnp.float32)
    up_local = jnp.einsum("rd,rf->df", rows_two, d_up, preferred_element_type=jnp.float32)
    d_normed_two = jnp.einsum("rf,df->rd", d_gate, gate_back, preferred_element_type=jnp.float32)
    d_normed_two = d_normed_two + jnp.einsum(
        "rf,df->rd", d_up, up_back, preferred_element_type=jnp.float32
    )
    norm_two_pull = jax.vjp(rms_norm, hidden, gain_two)[1]
    d_hidden_norm, d_gain_two = norm_two_pull(
        scatter_rows(d_normed_two.reshape(seq_count, span, width))
    )
    d_hidden = out_grad.astype(jnp.float32) + d_hidden_norm
    branch_rows = gather_rows(d_hidden.astype(jnp.bfloat16)).reshape(row_count, width)
    out_local = jnp.einsum("rd,rp->dp", branch_rows, mixed, preferred_element_type=jnp.float32)
    d_mixed = jnp.dot(branch_rows, out_back, preferred_element_type=jnp.float32).astype(
        jnp.bfloat16
    )
    d_mixed = d_mixed.reshape(seq_count, span, local_heads, HEAD)
    d_query_parts = []
    d_key_parts = []
    d_value_parts = []
    d_bias = jnp.zeros((2, local_heads), jnp.float32)
    for seq in range(seq_count):
        key_rows = keys_all[seq].reshape(seq_length, local_heads, HEAD)
        value_rows = values_all[seq].reshape(seq_length, local_heads, HEAD)

        def back_block(carry, item, seq=seq, key_rows=key_rows, value_rows=value_rows):
            d_keys, d_values, bias_sum = carry
            first, lse_block = item
            query_block = queries[seq]
            query_var = my_variates[seq]
            query_seg = my_segments[seq]
            scores, same = scores_of(
                query_block, key_rows, query_var, variate_ids[seq], query_seg, segment_ids[seq]
            )
            probs = jnp.exp(scores - lse_block[:, :, None])
            probs_low = probs.astype(jnp.bfloat16)
            d_out = d_mixed[seq]
            d_probs = jnp.einsum(
                "qhd,khd->hqk", d_out, value_rows, preferred_element_type=jnp.float32
            )
            delta = jnp.sum(probs * d_probs, axis=-1, keepdims=True)
            d_scores = (probs * (d_probs - delta)).astype(jnp.bfloat16)
            d_query = (
                jnp.einsum("hqk,khd->qhd", d_scores, key_rows, preferred_element_type=jnp.float32)
                * scale
            )
            d_keys = (
                d_keys
                + jnp.einsum(
                    "hqk,qhd->khd", d_scores, query_block, preferred_element_type=jnp.float32
                )
                * scale
            )
            d_values = d_values + jnp.einsum(
                "hqk,qhd->khd", probs_low, d_out, preferred_element_type=jnp.float32
            )
            wide_scores = d_scores.astype(jnp.float32)
            same_sum = jnp.sum(jnp.where(same, wide_scores, 0.0), axis=(1, 2))
            diff_sum = jnp.sum(jnp.where(same, 0.0, wide_scores), axis=(1, 2))
            return ((d_keys, d_values, bias_sum + jnp.stack([same_sum, diff_sum])), d_query)

        zero_rows = jnp.zeros((seq_length, local_heads, HEAD), jnp.float32)
        (d_keys, d_values, bias_sum), d_query_blocks = lax.scan(
            back_block,
            (zero_rows, zero_rows, jnp.zeros((2, local_heads), jnp.float32)),
            (block_starts, lse_parts[seq]),
        )
        d_query_parts.append(d_query_blocks.reshape(span, local_heads, HEAD))
        d_key_parts.append(d_keys.reshape(seq_length, proj_width))
        d_value_parts.append(d_values.reshape(seq_length, proj_width))
        d_bias = d_bias + bias_sum
    d_keys_mine, d_values_mine = (
        lax.psum_scatter(
            jnp.stack(d_key_parts).astype(jnp.bfloat16), "ctx", scatter_dimension=1, tiled=True
        ).astype(jnp.float32),
        lax.psum_scatter(
            jnp.stack(d_value_parts).astype(jnp.bfloat16), "ctx", scatter_dimension=1, tiled=True
        ).astype(jnp.float32),
    )

    def rope_local(values):
        return rotate(values, my_times)

    rope_pull = jax.vjp(rope_local, queries_raw)[1]
    d_query_raw = (
        rope_pull(jnp.stack(d_query_parts))[0].astype(jnp.bfloat16).reshape(row_count, proj_width)
    )
    d_key_raw = (
        rope_pull(d_keys_mine.reshape(seq_count, span, local_heads, HEAD))[0]
        .astype(jnp.bfloat16)
        .reshape(row_count, proj_width)
    )
    d_value_low = d_values_mine.astype(jnp.bfloat16).reshape(row_count, proj_width)
    query_local = jnp.einsum("rd,rp->dp", rows_one, d_query_raw, preferred_element_type=jnp.float32)
    key_local = jnp.einsum("rd,rp->dp", rows_one, d_key_raw, preferred_element_type=jnp.float32)
    value_local = jnp.einsum("rd,rp->dp", rows_one, d_value_low, preferred_element_type=jnp.float32)
    d_normed_one = jnp.einsum(
        "rp,dp->rd", d_query_raw, query_back, preferred_element_type=jnp.float32
    )
    d_normed_one = d_normed_one + jnp.einsum(
        "rp,dp->rd", d_key_raw, key_back, preferred_element_type=jnp.float32
    )
    d_normed_one = d_normed_one + jnp.einsum(
        "rp,dp->rd", d_value_low, value_back, preferred_element_type=jnp.float32
    )
    norm_one_pull = jax.vjp(rms_norm, inputs, gain_one)[1]
    d_input_norm, d_gain_one = norm_one_pull(
        scatter_rows(d_normed_one.reshape(seq_count, span, width))
    )
    in_grad = (d_hidden + d_input_norm).astype(jnp.bfloat16)
    query_grad, key_grad, value_grad, out_weight_grad = (
        lax.psum_scatter(
            query_local.astype(jnp.bfloat16), ("fsdp", "ctx"), scatter_dimension=0, tiled=True
        ).astype(jnp.float32),
        lax.psum_scatter(
            key_local.astype(jnp.bfloat16), ("fsdp", "ctx"), scatter_dimension=0, tiled=True
        ).astype(jnp.float32),
        lax.psum_scatter(
            value_local.astype(jnp.bfloat16), ("fsdp", "ctx"), scatter_dimension=0, tiled=True
        ).astype(jnp.float32),
        lax.psum_scatter(
            out_local.astype(jnp.bfloat16), ("fsdp", "ctx"), scatter_dimension=0, tiled=True
        ).astype(jnp.float32),
    )
    gate_grad, up_grad, down_grad = (
        lax.psum_scatter(
            gate_local.astype(jnp.bfloat16), ("fsdp", "ctx"), scatter_dimension=0, tiled=True
        ).astype(jnp.float32),
        lax.psum_scatter(
            up_local.astype(jnp.bfloat16), ("fsdp", "ctx"), scatter_dimension=0, tiled=True
        ).astype(jnp.float32),
        lax.psum_scatter(
            down_local.astype(jnp.bfloat16), ("fsdp", "ctx"), scatter_dimension=0, tiled=True
        ).astype(jnp.float32),
    )
    head_offset = lax.axis_index("tp") * local_heads
    bias_full = lax.dynamic_update_slice_in_dim(
        jnp.zeros((2, HEADS), jnp.float32), d_bias, head_offset, 1
    )
    attn_gain_grad, ffn_gain_grad, bias_total = lax.psum(
        (d_gain_one, d_gain_two, bias_full), ("fsdp", "ctx", "tp")
    )
    bias_grad = lax.dynamic_slice_in_dim(bias_total, head_offset, local_heads, 1)
    return (
        layer_out,
        in_grad,
        attn_gain_grad,
        ffn_gain_grad,
        query_grad,
        key_grad,
        value_grad,
        out_weight_grad,
        bias_grad,
        gate_grad,
        up_grad,
        down_grad,
    )


def solution(mesh):
    in_specs = (
        P("fsdp", ("ctx", "tp"), None),
        P(),
        P(),
        P(("fsdp", "ctx"), "tp"),
        P(("fsdp", "ctx"), "tp"),
        P(("fsdp", "ctx"), "tp"),
        P(("fsdp", "ctx"), "tp"),
        P(None, "tp"),
        P(("fsdp", "ctx"), "tp"),
        P(("fsdp", "ctx"), "tp"),
        P(("fsdp", "ctx"), "tp"),
        P("fsdp", None),
        P("fsdp", None),
        P("fsdp", None),
        P("fsdp", ("ctx", "tp"), None),
    )
    out_specs = (
        P("fsdp", ("ctx", "tp"), None),
        P("fsdp", ("ctx", "tp"), None),
        P(),
        P(),
        P(("fsdp", "ctx"), "tp"),
        P(("fsdp", "ctx"), "tp"),
        P(("fsdp", "ctx"), "tp"),
        P(("fsdp", "ctx"), "tp"),
        P(None, "tp"),
        P(("fsdp", "ctx"), "tp"),
        P(("fsdp", "ctx"), "tp"),
        P(("fsdp", "ctx"), "tp"),
    )
    return jax.shard_map(shards, mesh=mesh, in_specs=in_specs, out_specs=out_specs, check_vma=False)
```

profile of v0, /device:TPU:0, one launch (start us, length us, event | category | flops | bytes accessed | tf_op | source)
XLA Modules:
  0.0 1151.3 jit_solution(9747962312075755871)
XLA Ops:
  15.6 33.3 %all_gather.49 = bf16[1024,256]{1,0:T(8,128)(2,1)S(1)} all-gather(bf16[128,256]{1,0:T(8,128)(2,1)} %param.18), channel_id=1, replica_groups=mesh['fsdp'=4,'ctx'=2,'tp'=4] {'fsdp','ctx'}, dimensions={0}, use_global_device_ids=true | all-gather | bytes 589824 | tf_op jit(solution)/shard_map/all_gather | solution.py:81
  48.9 31.6 %all_gather.50 = bf16[1024,256]{1,0:T(8,128)(2,1)S(1)} all-gather(bf16[128,256]{1,0:T(8,128)(2,1)} %param.19), channel_id=1, replica_groups=mesh['fsdp'=4,'ctx'=2,'tp'=4] {'fsdp','ctx'}, dimensions={0}, use_global_device_ids=true | all-gather | bytes 589824 | tf_op jit(solution)/shard_map/all_gather | solution.py:82
  80.5 31.9 %all_gather.47 = bf16[1024,256]{1,0:T(8,128)(2,1)S(1)} all-gather(bf16[128,256]{1,0:T(8,128)(2,1)} %param.20), channel_id=1, replica_groups=mesh['fsdp'=4,'ctx'=2,'tp'=4] {'fsdp','ctx'}, dimensions={0}, use_global_device_ids=true | all-gather | bytes 589824 | tf_op jit(solution)/shard_map/all_gather | solution.py:83
  112.3 31.6 %all_gather.52 = bf16[1024,256]{1,0:T(8,128)(2,1)S(1)} all-gather(bf16[128,256]{1,0:T(8,128)(2,1)} %param.21), channel_id=1, replica_groups=mesh['fsdp'=4,'ctx'=2,'tp'=4] {'fsdp','ctx'}, dimensions={0}, use_global_device_ids=true | all-gather | bytes 589824 | tf_op jit(solution)/shard_map/all_gather | solution.py:84
  156.3 14.2 %all-gather.12.cloned.1.call-done = bf16[2,1024,256]{2,1,0:T(8,128)(2,1)} async-done(((bf16[2,512,256]{2,1,0:T(8,128)(2,1)}), bf16[2,1024,256]{2,1,0:T(8,128)(2,1)}) %all-gather.12.cloned.1.call-update) | async-done | bytes 1048592 | tf_op jit(solution)/shard_map/all_gather | solution.py:101
  176.9 17.1 %all-gather.14.cloned.1.call-done = bf16[2,1024,256]{1,2,0:T(8,128)(2,1)} async-done(((bf16[2,512,256]{1,2,0:T(8,128)(2,1)}), bf16[2,1024,256]{1,2,0:T(8,128)(2,1)}) %all-gather.14.cloned.1.call-update) | async-done | bytes 1048592 | tf_op jit(solution)/shard_map/all_gather | solution.py:100
  221.1 43.6 %reduce-scatter.16.cloned.1.call-done = f32[2,128,1024]{2,1,0:T(8,128)} async-done(((f32[2,512,1024]{2,1,0:T(8,128)}), f32[2,128,1024]{2,1,0:T(8,128)}) %reduce-scatter.16.cloned.1.call-update) | async-done | bytes 1048592 | tf_op jit(solution)/shard_map/reduce_scatter | solution.py:39
  272.2 23.0 %all-gather.16.cloned.1.call-done = bf16[2,512,1024]{2,1,0:T(8,128)(2,1)} async-done(((bf16[2,128,1024]{2,1,0:T(8,128)(2,1)}), bf16[2,512,1024]{2,1,0:T(8,128)(2,1)}) %all-gather.16.cloned.1.call-update) | async-done | bytes 2097168 | tf_op jit(solution)/shard_map/all_gather | solution.py:35
  295.3 6.6 fusion.72
  301.8 45.0 %all-gather.18.cloned.1.call-done = bf16[1024,1024]{1,0:T(8,128)(2,1)} async-done(((bf16[128,1024]{1,0:T(8,128)(2,1)}), bf16[1024,1024]{1,0:T(8,128)(2,1)}) %all-gather.18.cloned.1.call-update) | async-done | bytes 2097168 | tf_op jit(solution)/shard_map/all_gather | solution.py:148
  346.9 6.5 fusion.71
  353.4 16.1 %all-gather.24.cloned.1.call-done = bf16[2,512,1024]{2,1,0:T(8,128)(2,1)} async-done(((bf16[2,128,1024]{2,1,0:T(8,128)(2,1)}), bf16[2,512,1024]{2,1,0:T(8,128)(2,1)}) %all-gather.24.cloned.1.call-update) | async-done | bytes 2097168 | tf_op jit(solution)/shard_map/all_gather | solution.py:35
  369.5 51.7 %all-gather.22.cloned.1.call-done = bf16[1024,1024]{1,0:T(8,128)(2,1)} async-done(((bf16[128,1024]{1,0:T(8,128)(2,1)}), bf16[1024,1024]{1,0:T(8,128)(2,1)}) %all-gather.22.cloned.1.call-update) | async-done | bytes 2097168 | tf_op jit(solution)/shard_map/all_gather | solution.py:150
  421.2 9.9 multiply_convert_fusion.2
  438.7 43.1 %reduce-scatter.20.cloned.1.call-done = f32[2,128,1024]{2,1,0:T(8,128)} async-done(((f32[2,512,1024]{2,1,0:T(8,128)}), f32[2,128,1024]{2,1,0:T(8,128)}) %reduce-scatter.20.cloned.1.call-update) | async-done | bytes 1048592 | tf_op jit(solution)/shard_map/reduce_scatter | solution.py:39
  486.5 22.2 %all-gather.26.cloned.1.call-done = bf16[2,512,1024]{2,1,0:T(8,128)(2,1)} async-done(((bf16[2,128,1024]{2,1,0:T(8,128)(2,1)}), bf16[2,512,1024]{2,1,0:T(8,128)(2,1)}) %all-gather.26.cloned.1.call-update) | async-done | bytes 2097168 | tf_op jit(solution)/shard_map/all_gather | solution.py:35
  511.2 5.8 fusion.24
  517.1 7.2 multiply_reduce_fusion.1
  533.1 8.7 fusion
  554.9 6.0 convert_bitcast_fusion
  565.0 5.9 convolution_convert_fusion
  571.0 5.9 convolution_convert_fusion.1
  611.5 6.7 fusion.73
  618.3 29.3 %reduce-scatter.40.cloned.1.call-done = bf16[128,1024]{1,0:T(8,128)(2,1)} async-done(((bf16[1024,1024]{1,0:T(8,128)(2,1)}), bf16[128,1024]{1,0:T(8,128)(2,1)}) %reduce-scatter.40.cloned.1.call-update) | async-done | bytes 262160
  649.6 68.4 %reduce-scatter.38.cloned.1.call-done = bf16[128,1024]{1,0:T(8,128)(2,1)} async-done(((bf16[1024,1024]{1,0:T(8,128)(2,1)}), bf16[128,1024]{1,0:T(8,128)(2,1)}) %reduce-scatter.38.cloned.1.call-update) | async-done | bytes 262160 | tf_op jit(solution)/shard_map/reduce_scatter | solution.py:305
  719.8 68.3 %reduce-scatter.36.cloned.1.call-done = bf16[128,1024]{1,0:T(8,128)(2,1)} async-done(((bf16[1024,1024]{1,0:T(8,128)(2,1)}), bf16[128,1024]{1,0:T(8,128)(2,1)}) %reduce-scatter.36.cloned.1.call-update) | async-done | bytes 262160 | tf_op jit(solution)/shard_map/reduce_scatter | solution.py:302
  790.1 62.4 %reduce-scatter.34.cloned.1.call-done = bf16[128,256]{1,0:T(8,128)(2,1)} async-done(((bf16[1024,256]{1,0:T(8,128)(2,1)}), bf16[128,256]{1,0:T(8,128)(2,1)}) %reduce-scatter.34.cloned.1.call-update) | async-done | bytes 65552 | tf_op jit(solution)/shard_map/reduce_scatter | solution.py:297
  854.0 63.0 %reduce-scatter.32.cloned.1.call-done = bf16[128,256]{1,0:T(8,128)(2,1)} async-done(((bf16[1024,256]{1,0:T(8,128)(2,1)}), bf16[128,256]{1,0:T(8,128)(2,1)}) %reduce-scatter.32.cloned.1.call-update) | async-done | bytes 65552 | tf_op jit(solution)/shard_map/reduce_scatter | solution.py:294
  918.5 63.3 %reduce-scatter.30.cloned.1.call-done = bf16[128,256]{1,0:T(8,128)(2,1)} async-done(((bf16[1024,256]{1,0:T(8,128)(2,1)}), bf16[128,256]{1,0:T(8,128)(2,1)}) %reduce-scatter.30.cloned.1.call-update) | async-done | bytes 65552 | tf_op jit(solution)/shard_map/reduce_scatter | solution.py:291
  983.4 63.6 %reduce-scatter.28.cloned.1.call-done = bf16[128,256]{1,0:T(8,128)(2,1)} async-done(((bf16[1024,256]{1,0:T(8,128)(2,1)}), bf16[128,256]{1,0:T(8,128)(2,1)}) %reduce-scatter.28.cloned.1.call-update) | async-done | bytes 65552 | tf_op jit(solution)/shard_map/reduce_scatter | solution.py:288
  1048.4 44.4 %reduce-scatter.26.cloned.1.call-done = f32[2,128,1024]{2,1,0:T(8,128)} async-done(((f32[2,512,1024]{2,1,0:T(8,128)}), f32[2,128,1024]{2,1,0:T(8,128)}) %reduce-scatter.26.cloned.1.call-update) | async-done | bytes 1048592 | tf_op jit(solution)/shard_map/reduce_scatter | solution.py:39
  1094.4 39.8 %all-reduce.4 = (f32[1024]{0:T(1024)}, f32[1024]{0:T(1024)}, f32[2,16]{1,0:T(2,128)S(1)}) all-reduce(f32[1024]{0:T(1024)S(1)} %get-tuple-element.206, f32[1024]{0:T(1024)S(1)} %copy-done.44, f32[2,16]{1,0:T(2,128)S(1)} %dynamic_update_slice.18), channel_id=1, replica_groups=mesh['fsdp'=4,'ctx'=2,'tp'=4] {'fsdp','ctx','tp'}, use_global_device_ids=true, to_apply=%region_17.18 | all-reduce | flops 2080 | bytes 16640 | tf_op jit(solution)/shard_map/psum | solution.py:316
  (275 shorter events, 158.0 us)
Async XLA Ops:
  8.0 136.9 %all-gather.10.cloned.1.call-start = ((), (), s32[]{:S(2)}) async-start(), calls=%async_computation.13 | async-start | bytes 2621440 | tf_op jit(solution)/shard_map/all_gather | solution.py:35
  13.2 157.4 %all-gather.12.cloned.1.call-start = ((), (), s32[]{:S(2)}) async-start(), calls=%async_computation.14 | async-start | bytes 1572864 | tf_op jit(solution)/shard_map/all_gather | solution.py:101
  148.2 45.8 %all-gather.14.cloned.1.call-start = ((), (), s32[]{:S(2)}) async-start(), calls=%async_computation.15 | async-start | bytes 1572864 | tf_op jit(solution)/shard_map/all_gather | solution.py:100
  153.4 111.4 %reduce-scatter.16.cloned.1.call-start = ((), (), s32[]{:S(2)}) async-start(), calls=%async_computation.16 | async-start | bytes 5242880 | tf_op jit(solution)/shard_map/reduce_scatter | solution.py:39
  220.0 52.2 %all-gather.20.cloned.1.call-start = ((), (), s32[]{:S(2)}) async-start(), calls=%async_computation.19 | async-start | bytes 2359296 | tf_op jit(solution)/shard_map/all_gather | solution.py:149
  220.6 74.7 %all-gather.16.cloned.1.call-start = ((), (), s32[]{:S(2)}) async-start(), calls=%async_computation.17 | async-start | bytes 2621440 | tf_op jit(solution)/shard_map/all_gather | solution.py:35
  221.1 262.7 %copy-start.31 = (f32[1024]{0:T(1024)}, f32[1024]{0:T(1024)S(1)}, u32[]{:S(2)}) copy-start(f32[1024]{0:T(1024)S(1)} %convert_element_type.167) | copy-start | bytes 12292
  266.2 217.6 %copy-start.41 = (f32[2,128]{1,0:T(2,128)}, f32[2,128]{1,0:T(2,128)S(1)}, u32[]{:S(2)}) copy-start(f32[2,128]{1,0:T(2,128)S(1)} %fusion.57) | copy-start | bytes 3076
  267.2 79.7 %all-gather.18.cloned.1.call-start = ((), (), s32[]{:S(2)}) async-start(), calls=%async_computation.18 | async-start | bytes 2359296 | tf_op jit(solution)/shard_map/all_gather | solution.py:148
  267.8 101.7 %all-gather.24.cloned.1.call-start = ((), (), s32[]{:S(2)}) async-start(), calls=%async_computation.22 | async-start | bytes 2621440 | tf_op jit(solution)/shard_map/all_gather | solution.py:35
  268.5 152.7 %all-gather.22.cloned.1.call-start = ((), (), s32[]{:S(2)}) async-start(), calls=%async_computation.20 | async-start | bytes 2359296 | tf_op jit(solution)/shard_map/all_gather | solution.py:150
  269.3 212.5 %reduce-scatter.20.cloned.1.call-start = ((), (), s32[]{:S(2)}) async-start(), calls=%async_computation.23 | async-start | bytes 5242880 | tf_op jit(solution)/shard_map/reduce_scatter | solution.py:39
  438.6 70.1 %all-gather.26.cloned.1.call-start = ((), (), s32[]{:S(2)}) async-start(), calls=%async_computation.24 | async-start | bytes 2621440 | tf_op jit(solution)/shard_map/all_gather | solution.py:35
  486.2 98.6 %reduce-scatter.24.cloned.1.call-start = ((), (), s32[]{:S(2)}) async-start(), calls=%async_computation.26 | async-start | bytes 1572864 | tf_op jit(solution)/shard_map/reduce_scatter | solution.py:252
  533.0 59.9 %reduce-scatter.22.cloned.1.call-start = ((), (), s32[]{:S(2)}) async-start(), calls=%async_computation.25 | async-start | bytes 1572864 | tf_op jit(solution)/shard_map/reduce_scatter | solution.py:249
  554.6 93.0 %reduce-scatter.40.cloned.1.call-start = ((), (), s32[]{:S(2)}) async-start(), calls=%async_computation.34 | async-start | bytes 2359296
  564.9 153.1 %reduce-scatter.38.cloned.1.call-start = ((), (), s32[]{:S(2)}) async-start(), calls=%async_computation.33 | async-start | bytes 2359296 | tf_op jit(solution)/shard_map/reduce_scatter | solution.py:305
  570.9 217.2 %reduce-scatter.36.cloned.1.call-start = ((), (), s32[]{:S(2)}) async-start(), calls=%async_computation.32 | async-start | bytes 2359296 | tf_op jit(solution)/shard_map/reduce_scatter | solution.py:302
  576.9 275.5 %reduce-scatter.34.cloned.1.call-start = ((), (), s32[]{:S(2)}) async-start(), calls=%async_computation.31 | async-start | bytes 589824 | tf_op jit(solution)/shard_map/reduce_scatter | solution.py:297
  580.2 336.8 %reduce-scatter.32.cloned.1.call-start = ((), (), s32[]{:S(2)}) async-start(), calls=%async_computation.30 | async-start | bytes 589824 | tf_op jit(solution)/shard_map/reduce_scatter | solution.py:294
  588.0 393.8 %reduce-scatter.30.cloned.1.call-start = ((), (), s32[]{:S(2)}) async-start(), calls=%async_computation.29 | async-start | bytes 589824 | tf_op jit(solution)/shard_map/reduce_scatter | solution.py:291
  600.0 447.0 %reduce-scatter.28.cloned.1.call-start = ((), (), s32[]{:S(2)}) async-start(), calls=%async_computation.28 | async-start | bytes 589824 | tf_op jit(solution)/shard_map/reduce_scatter | solution.py:288
  605.9 486.9 %reduce-scatter.26.cloned.1.call-start = ((), (), s32[]{:S(2)}) async-start(), calls=%async_computation.27 | async-start | bytes 5242880 | tf_op jit(solution)/shard_map/reduce_scatter | solution.py:39
  611.5 529.1 %reduce-scatter.18.cloned.1.call-start = ((), (), s32[]{:S(2)}) async-start(), calls=%async_computation.21 | async-start | bytes 5242880 | tf_op jit(solution)/shard_map/reduce_scatter | solution.py:39
  618.2 474.6 %copy-start.34 = (f32[1024]{0:T(1024)S(1)}, f32[1024]{0:T(1024)}, u32[]{:S(2)}) copy-start(f32[1024]{0:T(1024)} %copy-done.33) | copy-start | bytes 12292
  618.2 474.6 %copy-start.46 = (f32[2,128]{1,0:T(2,128)S(1)}, f32[2,128]{1,0:T(2,128)}, u32[]{:S(2)}) copy-start(f32[2,128]{1,0:T(2,128)} %copy-done.45) | copy-start | bytes 3076
  618.2 476.2 %copy-start.44 = (f32[1024]{0:T(1024)S(1)}, f32[1024]{0:T(1024)}, u32[]{:S(2)}) copy-start(f32[1024]{0:T(1024)} %get-tuple-element.204) | copy-start | bytes 12292
  618.2 516.6 %copy-start.48 = (f32[2,128]{1,0:T(2,128)S(1)}, f32[2,128]{1,0:T(2,128)}, u32[]{:S(2)}) copy-start(f32[2,128]{1,0:T(2,128)} %copy-done.47) | copy-start | bytes 3076
  618.2 522.4 %copy-start.5 = (f32[2,128,1024]{2,1,0:T(8,128)S(1)}, f32[2,128,1024]{2,1,0:T(8,128)}, u32[]{:S(2)}) copy-start(f32[2,128,1024]{2,1,0:T(8,128)} %reduce-scatter.20.cloned.1.call-done) | copy-start | bytes 3145732
  618.3 522.4 %copy-start.32 = (f32[1024]{0:T(1024)S(1)}, f32[1024]{0:T(1024)}, u32[]{:S(2)}) copy-start(f32[1024]{0:T(1024)} %copy-done.31) | copy-start | bytes 12292
  618.3 522.4 %copy-start.42 = (f32[2,128]{1,0:T(2,128)S(1)}, f32[2,128]{1,0:T(2,128)}, u32[]{:S(2)}) copy-start(f32[2,128]{1,0:T(2,128)} %copy-done.41) | copy-start | bytes 3076
  618.3 522.4 %copy-start.50 = (f32[2,128]{1,0:T(2,128)S(1)}, f32[2,128]{1,0:T(2,128)}, u32[]{:S(2)}) copy-start(f32[2,128]{1,0:T(2,128)} %copy-done.49) | copy-start | bytes 3076
  (57 other events, 1265.2 us)
Sparse Core Ops, SparseCore 0:
  13.3 25.2 all-gather.9
  148.3 22.1 all-gather.11
  172.7 21.2 all-gather.13
  220.1 44.5 reduce-scatter.15
  438.7 42.9 reduce-scatter.19
  533.1 20.3 reduce-scatter.23
  555.8 20.3 reduce-scatter.21
  579.7 67.8 reduce-scatter.39
  651.1 66.8 reduce-scatter.37
  721.4 66.6 reduce-scatter.35
  791.5 60.9 reduce-scatter.33
  856.0 60.9 reduce-scatter.31
  920.9 60.8 reduce-scatter.29
  986.0 60.9 reduce-scatter.27
  1049.3 43.4 reduce-scatter.25
  1095.4 45.2 reduce-scatter.17
Sparse Core Ops, SparseCore 1:
  222.9 49.3 all-gather.19
  274.3 20.9 all-gather.15
  297.5 49.3 all-gather.17
  348.5 20.9 all-gather.23
  371.8 49.3 all-gather.21
  486.3 22.4 all-gather.25
where the time goes:
time: 1160 us; the launch traced here: 1150 us
  waiting for transfers between devices  750 us (65%)
  blocking collectives  168 us (14%)
  matrix products  124 us (11%)
  other arithmetic  56.5 us (5%)
  local copies, waits for them, and re-layouts  33 us (3%)
  between operations  16.9 us (1%)
    reduce_scatter x4, waiting for transfers between devices, scatter_rows(): return lax.psum_scatter(values, 'tp', scatter_dimension=1, tiled=True)  137 us
    reduce_scatter x1, waiting for transfers between devices, shards(): lax.psum_scatter(up_local.astype(jnp.bfloat16), ('fsdp', 'ctx'), scatter_...  68.4 us
    reduce_scatter x1, waiting for transfers between devices, shards(): lax.psum_scatter(gate_local.astype(jnp.bfloat16), ('fsdp', 'ctx'), scatte...  68.3 us
    reduce_scatter x1, waiting for transfers between devices, shards(): lax.psum_scatter(query_local.astype(jnp.bfloat16), ('fsdp', 'ctx'), scatt...  63.6 us
    reduce_scatter x1, waiting for transfers between devices, shards(): lax.psum_scatter(key_local.astype(jnp.bfloat16), ('fsdp', 'ctx'), scatter...  63.3 us
    reduce_scatter x1, waiting for transfers between devices, shards(): lax.psum_scatter(value_local.astype(jnp.bfloat16), ('fsdp', 'ctx'), scatt...  63 us
    reduce_scatter x1, waiting for transfers between devices, shards(): lax.psum_scatter(out_local.astype(jnp.bfloat16), ('fsdp', 'ctx'), scatter...  62.4 us
    all_gather x4, waiting for transfers between devices, gather_rows(): return lax.all_gather(values, 'tp', axis=1, tiled=True)  61.4 us
  transfers between devices with their start and end apart: 22, of which 19 were waited for; matrix products, arithmetic and copies ran while one was open for 11% of the time, Pallas kernels for 0%

commit v1 on v0

--- a/solution.py
+++ b/solution.py
@@ -314,7 +314,7 @@
         jnp.zeros((2, HEADS), jnp.float32), d_bias, head_offset, 1
     )
     attn_gain_grad, ffn_gain_grad, bias_total = lax.psum(
-        (d_gain_one, d_gain_two, bias_full), ("fsdp", "ctx", "tp")
+        lax.psum((d_gain_one, d_gain_two, bias_full), ("ctx", "tp")), "fsdp"
     )
     bias_grad = lax.dynamic_slice_in_dim(bias_total, head_offset, local_heads, 1)
     return (

time: 1160 us -> 1160 us (level)
  blocking collectives: 168 us -> 154 us
  waiting for transfers between devices: 750 us -> 763 us
    psum x1 -> x2, blocking collectives: 39.8 us -> 25.8 us  [the longest x1 13.2 us: shards(): lax.psum((d_gain_one, d_gain_two, bias_full), ('ctx', 'tp'))]
    reduce_scatter x4, waiting for transfers between devices: 137 us -> 150 us  [scatter_rows(): return lax.psum_scatter(values, 'tp', scatter_dimension=1, tiled=True)]
where the time goes in v1:
time: 1160 us; the launch traced here: 1150 us
  waiting for transfers between devices  763 us (66%)
  blocking collectives  154 us (13%)
  matrix products  124 us (11%)
  other arithmetic  56.5 us (5%)
  local copies, waits for them, and re-layouts  33 us (3%)
  between operations  16.7 us (1%)
    reduce_scatter x4, waiting for transfers between devices, scatter_rows(): return lax.psum_scatter(values, 'tp', scatter_dimension=1, tiled=True)  150 us
    reduce_scatter x1, waiting for transfers between devices, shards(): lax.psum_scatter(gate_local.astype(jnp.bfloat16), ('fsdp', 'ctx'), scatte...  68.3 us
    reduce_scatter x1, waiting for transfers between devices, shards(): lax.psum_scatter(up_local.astype(jnp.bfloat16), ('fsdp', 'ctx'), scatter_...  68 us
    reduce_scatter x1, waiting for transfers between devices, shards(): lax.psum_scatter(query_local.astype(jnp.bfloat16), ('fsdp', 'ctx'), scatt...  63.6 us
    reduce_scatter x1, waiting for transfers between devices, shards(): lax.psum_scatter(key_local.astype(jnp.bfloat16), ('fsdp', 'ctx'), scatter...  63.4 us
    reduce_scatter x1, waiting for transfers between devices, shards(): lax.psum_scatter(value_local.astype(jnp.bfloat16), ('fsdp', 'ctx'), scatt...  63 us
    reduce_scatter x1, waiting for transfers between devices, shards(): lax.psum_scatter(out_local.astype(jnp.bfloat16), ('fsdp', 'ctx'), scatter...  62.4 us
    all_gather x4, waiting for transfers between devices, gather_rows(): return lax.all_gather(values, 'tp', axis=1, tiled=True)  61.2 us
  transfers between devices with their start and end apart: 22, of which 19 were waited for; matrix products, arithmetic and copies ran while one was open for 11% of the time, Pallas kernels for 0%

profile of v1, /device:TPU:0, one launch (start us, length us, event | category | flops | bytes accessed | tf_op | source)
XLA Modules:
  0.0 1149.6 jit_solution(5400061516866374129)
XLA Ops:
  15.6 33.3 %all_gather.49 = bf16[1024,256]{1,0:T(8,128)(2,1)S(1)} all-gather(bf16[128,256]{1,0:T(8,128)(2,1)} %param.18), channel_id=1, replica_groups=mesh['fsdp'=4,'ctx'=2,'tp'=4] {'fsdp','ctx'}, dimensions={0}, use_global_device_ids=true | all-gather | bytes 589824 | tf_op jit(solution)/shard_map/all_gather | solution.py:81
  49.0 31.6 %all_gather.50 = bf16[1024,256]{1,0:T(8,128)(2,1)S(1)} all-gather(bf16[128,256]{1,0:T(8,128)(2,1)} %param.19), channel_id=1, replica_groups=mesh['fsdp'=4,'ctx'=2,'tp'=4] {'fsdp','ctx'}, dimensions={0}, use_global_device_ids=true | all-gather | bytes 589824 | tf_op jit(solution)/shard_map/all_gather | solution.py:82
  80.5 31.9 %all_gather.47 = bf16[1024,256]{1,0:T(8,128)(2,1)S(1)} all-gather(bf16[128,256]{1,0:T(8,128)(2,1)} %param.20), channel_id=1, replica_groups=mesh['fsdp'=4,'ctx'=2,'tp'=4] {'fsdp','ctx'}, dimensions={0}, use_global_device_ids=true | all-gather | bytes 589824 | tf_op jit(solution)/shard_map/all_gather | solution.py:83
  112.4 31.6 %all_gather.52 = bf16[1024,256]{1,0:T(8,128)(2,1)S(1)} all-gather(bf16[128,256]{1,0:T(8,128)(2,1)} %param.21), channel_id=1, replica_groups=mesh['fsdp'=4,'ctx'=2,'tp'=4] {'fsdp','ctx'}, dimensions={0}, use_global_device_ids=true | all-gather | bytes 589824 | tf_op jit(solution)/shard_map/all_gather | solution.py:84
  156.4 14.3 %all-gather.12.cloned.1.call-done = bf16[2,1024,256]{2,1,0:T(8,128)(2,1)} async-done(((bf16[2,512,256]{2,1,0:T(8,128)(2,1)}), bf16[2,1024,256]{2,1,0:T(8,128)(2,1)}) %all-gather.12.cloned.1.call-update) | async-done | bytes 1048592 | tf_op jit(solution)/shard_map/all_gather | solution.py:101
  176.9 17.2 %all-gather.14.cloned.1.call-done = bf16[2,1024,256]{1,2,0:T(8,128)(2,1)} async-done(((bf16[2,512,256]{1,2,0:T(8,128)(2,1)}), bf16[2,1024,256]{1,2,0:T(8,128)(2,1)}) %all-gather.14.cloned.1.call-update) | async-done | bytes 1048592 | tf_op jit(solution)/shard_map/all_gather | solution.py:100
  221.0 43.8 %reduce-scatter.16.cloned.1.call-done = f32[2,128,1024]{2,1,0:T(8,128)} async-done(((f32[2,512,1024]{2,1,0:T(8,128)}), f32[2,128,1024]{2,1,0:T(8,128)}) %reduce-scatter.16.cloned.1.call-update) | async-done | bytes 1048592 | tf_op jit(solution)/shard_map/reduce_scatter | solution.py:39
  272.3 23.0 %all-gather.16.cloned.1.call-done = bf16[2,512,1024]{2,1,0:T(8,128)(2,1)} async-done(((bf16[2,128,1024]{2,1,0:T(8,128)(2,1)}), bf16[2,512,1024]{2,1,0:T(8,128)(2,1)}) %all-gather.16.cloned.1.call-update) | async-done | bytes 2097168 | tf_op jit(solution)/shard_map/all_gather | solution.py:35
  295.3 6.6 fusion.72
  301.9 45.0 %all-gather.18.cloned.1.call-done = bf16[1024,1024]{1,0:T(8,128)(2,1)} async-done(((bf16[128,1024]{1,0:T(8,128)(2,1)}), bf16[1024,1024]{1,0:T(8,128)(2,1)}) %all-gather.18.cloned.1.call-update) | async-done | bytes 2097168 | tf_op jit(solution)/shard_map/all_gather | solution.py:148
  346.9 6.5 fusion.71
  353.4 16.1 %all-gather.24.cloned.1.call-done = bf16[2,512,1024]{2,1,0:T(8,128)(2,1)} async-done(((bf16[2,128,1024]{2,1,0:T(8,128)(2,1)}), bf16[2,512,1024]{2,1,0:T(8,128)(2,1)}) %all-gather.24.cloned.1.call-update) | async-done | bytes 2097168 | tf_op jit(solution)/shard_map/all_gather | solution.py:35
  369.5 51.7 %all-gather.22.cloned.1.call-done = bf16[1024,1024]{1,0:T(8,128)(2,1)} async-done(((bf16[128,1024]{1,0:T(8,128)(2,1)}), bf16[1024,1024]{1,0:T(8,128)(2,1)}) %all-gather.22.cloned.1.call-update) | async-done | bytes 2097168 | tf_op jit(solution)/shard_map/all_gather | solution.py:150
  421.3 9.9 multiply_convert_fusion.2
  438.7 43.1 %reduce-scatter.20.cloned.1.call-done = f32[2,128,1024]{2,1,0:T(8,128)} async-done(((f32[2,512,1024]{2,1,0:T(8,128)}), f32[2,128,1024]{2,1,0:T(8,128)}) %reduce-scatter.20.cloned.1.call-update) | async-done | bytes 1048592 | tf_op jit(solution)/shard_map/reduce_scatter | solution.py:39
  486.8 22.0 %all-gather.26.cloned.1.call-done = bf16[2,512,1024]{2,1,0:T(8,128)(2,1)} async-done(((bf16[2,128,1024]{2,1,0:T(8,128)(2,1)}), bf16[2,512,1024]{2,1,0:T(8,128)(2,1)}) %all-gather.26.cloned.1.call-update) | async-done | bytes 2097168 | tf_op jit(solution)/shard_map/all_gather | solution.py:35
  517.1 7.2 multiply_reduce_fusion.1
  533.2 8.7 fusion
  554.9 6.0 convert_bitcast_fusion
  570.9 5.9 convolution_convert_fusion.1
  611.4 6.7 fusion.73
  618.2 29.1 %reduce-scatter.40.cloned.1.call-done = bf16[128,1024]{1,0:T(8,128)(2,1)} async-done(((bf16[1024,1024]{1,0:T(8,128)(2,1)}), bf16[128,1024]{1,0:T(8,128)(2,1)}) %reduce-scatter.40.cloned.1.call-update) | async-done | bytes 262160
  649.4 68.0 %reduce-scatter.38.cloned.1.call-done = bf16[128,1024]{1,0:T(8,128)(2,1)} async-done(((bf16[1024,1024]{1,0:T(8,128)(2,1)}), bf16[128,1024]{1,0:T(8,128)(2,1)}) %reduce-scatter.38.cloned.1.call-update) | async-done | bytes 262160 | tf_op jit(solution)/shard_map/reduce_scatter | solution.py:305
  719.2 68.3 %reduce-scatter.36.cloned.1.call-done = bf16[128,1024]{1,0:T(8,128)(2,1)} async-done(((bf16[1024,1024]{1,0:T(8,128)(2,1)}), bf16[128,1024]{1,0:T(8,128)(2,1)}) %reduce-scatter.36.cloned.1.call-update) | async-done | bytes 262160 | tf_op jit(solution)/shard_map/reduce_scatter | solution.py:302
  789.5 62.4 %reduce-scatter.34.cloned.1.call-done = bf16[128,256]{1,0:T(8,128)(2,1)} async-done(((bf16[1024,256]{1,0:T(8,128)(2,1)}), bf16[128,256]{1,0:T(8,128)(2,1)}) %reduce-scatter.34.cloned.1.call-update) | async-done | bytes 65552 | tf_op jit(solution)/shard_map/reduce_scatter | solution.py:297
  853.3 63.0 %reduce-scatter.32.cloned.1.call-done = bf16[128,256]{1,0:T(8,128)(2,1)} async-done(((bf16[1024,256]{1,0:T(8,128)(2,1)}), bf16[128,256]{1,0:T(8,128)(2,1)}) %reduce-scatter.32.cloned.1.call-update) | async-done | bytes 65552 | tf_op jit(solution)/shard_map/reduce_scatter | solution.py:294
  917.8 63.4 %reduce-scatter.30.cloned.1.call-done = bf16[128,256]{1,0:T(8,128)(2,1)} async-done(((bf16[1024,256]{1,0:T(8,128)(2,1)}), bf16[128,256]{1,0:T(8,128)(2,1)}) %reduce-scatter.30.cloned.1.call-update) | async-done | bytes 65552 | tf_op jit(solution)/shard_map/reduce_scatter | solution.py:291
  982.7 63.6 %reduce-scatter.28.cloned.1.call-done = bf16[128,256]{1,0:T(8,128)(2,1)} async-done(((bf16[1024,256]{1,0:T(8,128)(2,1)}), bf16[128,256]{1,0:T(8,128)(2,1)}) %reduce-scatter.28.cloned.1.call-update) | async-done | bytes 65552 | tf_op jit(solution)/shard_map/reduce_scatter | solution.py:288
  1047.8 44.4 %reduce-scatter.26.cloned.1.call-done = f32[2,128,1024]{2,1,0:T(8,128)} async-done(((f32[2,512,1024]{2,1,0:T(8,128)}), f32[2,128,1024]{2,1,0:T(8,128)}) %reduce-scatter.26.cloned.1.call-update) | async-done | bytes 1048592 | tf_op jit(solution)/shard_map/reduce_scatter | solution.py:39
  1093.7 13.2 %all-reduce.4 = (f32[1024]{0:T(1024)S(1)}, f32[1024]{0:T(1024)S(1)}, f32[2,16]{1,0:T(2,128)S(1)}) all-reduce(f32[1024]{0:T(1024)S(1)} %get-tuple-element.206, f32[1024]{0:T(1024)S(1)} %copy-done.44, f32[2,16]{1,0:T(2,128)S(1)} %dynamic_update_slice.18), channel_id=1, replica_groups=mesh['fsdp'=4,'ctx'=2,'tp'=4] {'ctx','tp'}, use_global_device_ids=true, to_apply=%region_17.18 | all-reduce | flops 2080 | bytes 16640 | tf_op jit(solution)/shard_map/psum | solution.py:317
  1106.9 12.6 %all-reduce.5 = (f32[1024]{0:T(1024)}, f32[1024]{0:T(1024)}, f32[2,16]{1,0:T(2,128)S(1)}) all-reduce(f32[1024]{0:T(1024)S(1)} %get-tuple-element.224, f32[1024]{0:T(1024)S(1)} %get-tuple-element.225, f32[2,16]{1,0:T(2,128)S(1)} %get-tuple-element.226), channel_id=1, replica_groups=mesh['fsdp'=4,'ctx'=2,'tp'=4] {'fsdp'}, use_global_device_ids=true, to_apply=%region_18.19 | all-reduce | flops 2080 | bytes 16640 | tf_op jit(solution)/shard_map/psum | solution.py:316
  1120.2 19.1 %reduce-scatter.18.cloned.1.call-done = f32[2,128,1024]{2,1,0:T(8,128)} async-done(((f32[2,512,1024]{2,1,0:T(8,128)}), f32[2,128,1024]{2,1,0:T(8,128)}) %reduce-scatter.18.cloned.1.call-update) | async-done | bytes 1048592 | tf_op jit(solution)/shard_map/reduce_scatter | solution.py:39
  (276 shorter events, 163.9 us)
Async XLA Ops:
  8.0 136.9 %all-gather.10.cloned.1.call-start = ((), (), s32[]{:S(2)}) async-start(), calls=%async_computation.13 | async-start | bytes 2621440 | tf_op jit(solution)/shard_map/all_gather | solution.py:35
  13.2 157.4 %all-gather.12.cloned.1.call-start = ((), (), s32[]{:S(2)}) async-start(), calls=%async_computation.14 | async-start | bytes 1572864 | tf_op jit(solution)/shard_map/all_gather | solution.py:101
  148.3 45.8 %all-gather.14.cloned.1.call-start = ((), (), s32[]{:S(2)}) async-start(), calls=%async_computation.15 | async-start | bytes 1572864 | tf_op jit(solution)/shard_map/all_gather | solution.py:100
  153.4 111.4 %reduce-scatter.16.cloned.1.call-start = ((), (), s32[]{:S(2)}) async-start(), calls=%async_computation.16 | async-start | bytes 5242880 | tf_op jit(solution)/shard_map/reduce_scatter | solution.py:39
  220.1 52.2 %all-gather.20.cloned.1.call-start = ((), (), s32[]{:S(2)}) async-start(), calls=%async_computation.19 | async-start | bytes 2359296 | tf_op jit(solution)/shard_map/all_gather | solution.py:149
  220.7 74.7 %all-gather.16.cloned.1.call-start = ((), (), s32[]{:S(2)}) async-start(), calls=%async_computation.17 | async-start | bytes 2621440 | tf_op jit(solution)/shard_map/all_gather | solution.py:35
  221.0 262.9 %copy-start.31 = (f32[1024]{0:T(1024)}, f32[1024]{0:T(1024)S(1)}, u32[]{:S(2)}) copy-start(f32[1024]{0:T(1024)S(1)} %convert_element_type.167) | copy-start | bytes 12292
  266.3 217.6 %copy-start.41 = (f32[2,128]{1,0:T(2,128)}, f32[2,128]{1,0:T(2,128)S(1)}, u32[]{:S(2)}) copy-start(f32[2,128]{1,0:T(2,128)S(1)} %fusion.57) | copy-start | bytes 3076
  267.2 79.7 %all-gather.18.cloned.1.call-start = ((), (), s32[]{:S(2)}) async-start(), calls=%async_computation.18 | async-start | bytes 2359296 | tf_op jit(solution)/shard_map/all_gather | solution.py:148
  267.8 101.7 %all-gather.24.cloned.1.call-start = ((), (), s32[]{:S(2)}) async-start(), calls=%async_computation.22 | async-start | bytes 2621440 | tf_op jit(solution)/shard_map/all_gather | solution.py:35
  268.6 152.7 %all-gather.22.cloned.1.call-start = ((), (), s32[]{:S(2)}) async-start(), calls=%async_computation.20 | async-start | bytes 2359296 | tf_op jit(solution)/shard_map/all_gather | solution.py:150
  269.3 212.5 %reduce-scatter.20.cloned.1.call-start = ((), (), s32[]{:S(2)}) async-start(), calls=%async_computation.23 | async-start | bytes 5242880 | tf_op jit(solution)/shard_map/reduce_scatter | solution.py:39
  438.6 70.1 %all-gather.26.cloned.1.call-start = ((), (), s32[]{:S(2)}) async-start(), calls=%async_computation.24 | async-start | bytes 2621440 | tf_op jit(solution)/shard_map/all_gather | solution.py:35
  486.2 98.5 %reduce-scatter.24.cloned.1.call-start = ((), (), s32[]{:S(2)}) async-start(), calls=%async_computation.26 | async-start | bytes 1572864 | tf_op jit(solution)/shard_map/reduce_scatter | solution.py:252
  533.1 59.7 %reduce-scatter.22.cloned.1.call-start = ((), (), s32[]{:S(2)}) async-start(), calls=%async_computation.25 | async-start | bytes 1572864 | tf_op jit(solution)/shard_map/reduce_scatter | solution.py:249
  554.6 92.7 %reduce-scatter.40.cloned.1.call-start = ((), (), s32[]{:S(2)}) async-start(), calls=%async_computation.34 | async-start | bytes 2359296
  564.9 152.5 %reduce-scatter.38.cloned.1.call-start = ((), (), s32[]{:S(2)}) async-start(), calls=%async_computation.33 | async-start | bytes 2359296 | tf_op jit(solution)/shard_map/reduce_scatter | solution.py:305
  570.9 216.6 %reduce-scatter.36.cloned.1.call-start = ((), (), s32[]{:S(2)}) async-start(), calls=%async_computation.32 | async-start | bytes 2359296 | tf_op jit(solution)/shard_map/reduce_scatter | solution.py:302
  576.9 275.0 %reduce-scatter.34.cloned.1.call-start = ((), (), s32[]{:S(2)}) async-start(), calls=%async_computation.31 | async-start | bytes 589824 | tf_op jit(solution)/shard_map/reduce_scatter | solution.py:297
  580.1 336.3 %reduce-scatter.32.cloned.1.call-start = ((), (), s32[]{:S(2)}) async-start(), calls=%async_computation.30 | async-start | bytes 589824 | tf_op jit(solution)/shard_map/reduce_scatter | solution.py:294
  588.0 393.3 %reduce-scatter.30.cloned.1.call-start = ((), (), s32[]{:S(2)}) async-start(), calls=%async_computation.29 | async-start | bytes 589824 | tf_op jit(solution)/shard_map/reduce_scatter | solution.py:291
  599.9 446.4 %reduce-scatter.28.cloned.1.call-start = ((), (), s32[]{:S(2)}) async-start(), calls=%async_computation.28 | async-start | bytes 589824 | tf_op jit(solution)/shard_map/reduce_scatter | solution.py:288
  605.8 486.4 %reduce-scatter.26.cloned.1.call-start = ((), (), s32[]{:S(2)}) async-start(), calls=%async_computation.27 | async-start | bytes 5242880 | tf_op jit(solution)/shard_map/reduce_scatter | solution.py:39
  611.4 527.9 %reduce-scatter.18.cloned.1.call-start = ((), (), s32[]{:S(2)}) async-start(), calls=%async_computation.21 | async-start | bytes 5242880 | tf_op jit(solution)/shard_map/reduce_scatter | solution.py:39
  618.1 474.1 %copy-start.34 = (f32[1024]{0:T(1024)S(1)}, f32[1024]{0:T(1024)}, u32[]{:S(2)}) copy-start(f32[1024]{0:T(1024)} %copy-done.33) | copy-start | bytes 12292
  618.1 474.1 %copy-start.46 = (f32[2,128]{1,0:T(2,128)S(1)}, f32[2,128]{1,0:T(2,128)}, u32[]{:S(2)}) copy-start(f32[2,128]{1,0:T(2,128)} %copy-done.45) | copy-start | bytes 3076
  618.1 475.6 %copy-start.44 = (f32[1024]{0:T(1024)S(1)}, f32[1024]{0:T(1024)}, u32[]{:S(2)}) copy-start(f32[1024]{0:T(1024)} %get-tuple-element.204) | copy-start | bytes 12292
  618.1 502.1 %copy-start.48 = (f32[2,128]{1,0:T(2,128)S(1)}, f32[2,128]{1,0:T(2,128)}, u32[]{:S(2)}) copy-start(f32[2,128]{1,0:T(2,128)} %copy-done.47) | copy-start | bytes 3076
  618.1 521.1 %copy-start.5 = (f32[2,128,1024]{2,1,0:T(8,128)S(1)}, f32[2,128,1024]{2,1,0:T(8,128)}, u32[]{:S(2)}) copy-start(f32[2,128,1024]{2,1,0:T(8,128)} %reduce-scatter.20.cloned.1.call-done) | copy-start | bytes 3145732
  618.1 521.1 %copy-start.32 = (f32[1024]{0:T(1024)S(1)}, f32[1024]{0:T(1024)}, u32[]{:S(2)}) copy-start(f32[1024]{0:T(1024)} %copy-done.31) | copy-start | bytes 12292
  618.1 521.1 %copy-start.42 = (f32[2,128]{1,0:T(2,128)S(1)}, f32[2,128]{1,0:T(2,128)}, u32[]{:S(2)}) copy-start(f32[2,128]{1,0:T(2,128)} %copy-done.41) | copy-start | bytes 3076
  618.2 521.1 %copy-start.50 = (f32[2,128]{1,0:T(2,128)S(1)}, f32[2,128]{1,0:T(2,128)}, u32[]{:S(2)}) copy-start(f32[2,128]{1,0:T(2,128)} %copy-done.49) | copy-start | bytes 3076
  (57 other events, 1264.6 us)
Sparse Core Ops, SparseCore 0:
  13.3 25.2 all-gather.9
  148.4 22.1 all-gather.11
  172.7 21.2 all-gather.13
  220.2 44.5 reduce-scatter.15
  438.8 42.9 reduce-scatter.19
  533.2 20.3 reduce-scatter.23
  555.9 20.2 reduce-scatter.21
  579.7 67.5 reduce-scatter.39
  650.8 66.5 reduce-scatter.37
  720.8 66.6 reduce-scatter.35
  790.8 60.9 reduce-scatter.33
  855.4 60.9 reduce-scatter.31
  920.3 60.9 reduce-scatter.29
  985.3 60.8 reduce-scatter.27
  1048.6 43.4 reduce-scatter.25
  1094.7 44.4 reduce-scatter.17
Sparse Core Ops, SparseCore 1:
  222.9 49.3 all-gather.19
  274.4 20.9 all-gather.15
  297.5 49.3 all-gather.17
  348.6 20.9 all-gather.23
  371.9 49.3 all-gather.21
  486.3 22.4 all-gather.25
